TPU v7x, 32 devices: a whole 2x2x4 slice. The times are simulated.
32 devices in a mesh: occ: 4 (over y, x), vir: 8 (over z, core).
Axes of the slice: x: 2, y: 2, z: 4, core: 2. Of those that a mesh axis runs over, the one named last changes fastest.
Arguments:
- amplitudes: bfloat16 [1504, 3072], P('occ', 'vir'), may hold values from -6 to 6
- integrals: bfloat16 [3072, 3072], P(None, 'vir'), may hold values from -0.15625 to 0.15625
- tile_block: int32 [24], replicated, may hold values from 0 to 5, as said below
- pair_mask: int32 [6, 6], replicated, may hold values 0 or 1
- partner: int32 [1504], P('occ'), may hold values from 0 to 1503, as said below
Outputs:
- residual: float32 [1504, 3072], P('occ', 'vir')
Inputs may be any that keep to these rules, and one draw needn't show every extreme that they name: partner is an involution without fixed points: partner[partner[r]] = r and partner[r] != r. tile_block never falls along the tiles, and each of the 6 blocks holds at least one tile.
All inputs are finite; a program needn't handle non-finite values.
Results may differ from a plain program's by a relative error of at most 0.0003.
Values may be sent and summed in bfloat16 or wider, within the bound.
No kernel may reach another device: no remote copies, remote signals or barrier semaphores. Data moves between devices by JAX's collectives and lax.ppermute only.
A program may use at most 128 MiB of HBM per device.

v0:
```python
import jax
import jax.numpy as jnp
from jax import lax
from jax.sharding import PartitionSpec as P

TILE = 128


def body(amplitudes, integrals, tile_block, pair_mask, partner):
    columns = integrals.shape[1]
    local_tiles = columns // TILE
    total_tiles = tile_block.shape[0]
    groups = pair_mask.shape[0]
    first_tile = lax.axis_index("vir") * local_tiles
    own_blocks = lax.dynamic_slice_in_dim(tile_block, first_tile, local_tiles)
    labels = jnp.arange(groups, dtype=jnp.int32)
    row_onehot = (tile_block[:, None] == labels[None, :]).astype(jnp.float32)
    col_onehot = (own_blocks[:, None] == labels[None, :]).astype(jnp.float32)
    live_tiles = jnp.dot(jnp.dot(row_onehot, pair_mask.astype(jnp.float32)), col_onehot.T)
    masked = (
        integrals.reshape(total_tiles, TILE, local_tiles, TILE)
        * live_tiles.astype(jnp.bfloat16)[:, None, :, None]
    )
    masked = masked.reshape(integrals.shape)
    own_count = amplitudes.shape[0]
    gathered = lax.all_gather(amplitudes, "occ", axis=0, tiled=True)
    partner_rows = jnp.take(gathered, partner, axis=0)
    stacked = jnp.concatenate((amplitudes, partner_rows), axis=0)
    pair_sums = jnp.dot(
        lax.all_gather(stacked, "vir", axis=1, tiled=True),
        masked,
        preferred_element_type=jnp.float32,
    )
    residual = pair_sums[:own_count] - pair_sums[own_count:]
    return residual


def solution(mesh):
    placed = (P("occ", "vir"), P(None, "vir"), P(), P(), P("occ"))
    return jax.shard_map(
        body, mesh=mesh, in_specs=placed, out_specs=P("occ", "vir"), check_vma=False
    )
```

profile of v0, /device:TPU:0, one launch (start us, length us, event | category | flops | bytes accessed | tf_op | source)
XLA Modules:
  0.0 107.5 jit_solution(9422348159117418414)
XLA Ops:
  6.5 0.0 all-gather.3.cloned.1.call-start
  6.5 0.7 all-gather.3.cloned.1.call-update
  7.3 0.0 all-gather.5.cloned.1.call-start
  7.3 0.7 compare_select_fusion
  8.0 0.7 compare_and_fusion
  8.7 30.6 %all-gather.3.cloned.1.call-done = bf16[1504,384]{1,0:T(8,128)(2,1)} async-done(((bf16[376,384]{1,0:T(8,128)(2,1)}), bf16[1504,384]{1,0:T(8,128)(2,1)}) %all-gather.3.cloned.1.call-update) | async-done | bytes 1155088 | tf_op jit(solution)/shard_map/all_gather | solution.py:26
  39.3 3.4 %gather_fusion = bf16[376,384]{1,0:T(8,128)(2,1)S(1)} fusion(bf16[1504,384]{1,0:T(8,128)(2,1)} %all-gather.3.cloned.1.call-done, s32[1024]{0:T(1024)S(1)} %pad_clamp_fusion), kind=kCustom, calls=%fused_computation | custom fusion | bytes 579040 | tf_op jit(solution)/shard_map/jit(_take)/gather | solution.py:27
  42.7 0.1 broadcast_select_fusion
  42.9 0.0 copy-done.2
  42.9 0.9 pad_maximum_fusion
  43.7 0.0 all-gather.5.cloned.1.call-update
  43.8 0.0 copy-done
  43.8 0.0 copy-start.4
  43.8 0.0 copy-start.3
  43.8 2.6 %copy.7 = bf16[3072,384]{0,1:T(8,128)(2,1)} copy(bf16[3072,384]{1,0:T(8,128)(2,1)S(1)} %copy-done) | data formatting | bytes 4718592 | tf_op args[1]
  46.4 0.0 copy-done.4
  46.4 0.1 dynamic_slice.3
  46.5 0.0 copy-done.3
  46.5 0.3 fusion.5
  46.8 47.7 %all-gather.5.cloned.1.call-done = bf16[752,3072]{1,0:T(8,128)(2,1)} async-done(((bf16[752,384]{1,0:T(8,128)(2,1)}), bf16[752,3072]{1,0:T(8,128)(2,1)}) %all-gather.5.cloned.1.call-update) | async-done | bytes 4620304 | tf_op jit(solution)/shard_map/all_gather | solution.py:30
  94.5 0.4 mul.15
  94.9 0.0 copy-done.1
  94.9 4.9 %fusion = f32[752,384]{1,0:T(8,128)S(1)} fusion(bf16[752,3072]{1,0:T(8,128)(2,1)} %all-gather.5.cloned.1.call-done, bf16[3072,384]{0,1:T(8,128)(2,1)S(1)} %copy-done.1, bf16[48,8,24,128]{3,2,1,0:T(8,128)(2,1)S(1)} %bitcast.8), kind=kOutput, calls=%fused_computation.2 | convolution fusion | flops 1775370240 | bytes 10493952 | tf_op jit(solution)/shard_map/dot_general | solution.py:29
  99.8 0.9 slice_subtract_fusion
  (4 shorter events, 0.0 us)
Async XLA Ops:
  6.5 36.3 %copy-start.2 = (bf16[376,384]{1,0:T(8,128)(2,1)S(1)}, bf16[376,384]{1,0:T(8,128)(2,1)}, u32[]{:S(2)}) copy-start(bf16[376,384]{1,0:T(8,128)(2,1)} %param.5) | copy-start | bytes 866308
  6.5 32.8 %all-gather.3.cloned.1.call-start = ((), (), s32[]{:S(2)}) async-start(), calls=%async_computation | async-start | bytes 1443840 | tf_op jit(solution)/shard_map/all_gather | solution.py:26
  7.3 87.3 %all-gather.5.cloned.1.call-start = ((), (), s32[]{:S(2)}) async-start(), calls=%async_computation.1 | async-start | bytes 5197824 | tf_op jit(solution)/shard_map/all_gather | solution.py:30
  8.7 35.1 %copy-start = (bf16[3072,384]{1,0:T(8,128)(2,1)S(1)}, bf16[3072,384]{1,0:T(8,128)(2,1)}, u32[]{:S(2)}) copy-start(bf16[3072,384]{1,0:T(8,128)(2,1)} %param.6) | copy-start | bytes 7077892
  43.8 2.7 %copy-start.4 = (s32[24]{0:T(128)S(1)}, s32[24]{0:T(128)}, u32[]{:S(2)}) copy-start(s32[24]{0:T(128)} %param.7) | copy-start | bytes 292
  43.8 2.7 %copy-start.3 = (s32[6,6]{1,0:T(8,128)S(1)}, s32[6,6]{1,0:T(8,128)}, u32[]{:S(2)}) copy-start(s32[6,6]{1,0:T(8,128)} %param.8) | copy-start | bytes 436
  46.4 48.5 %copy-start.1 = (bf16[3072,384]{0,1:T(8,128)(2,1)S(1)}, bf16[3072,384]{0,1:T(8,128)(2,1)}, u32[]{:S(2)}) copy-start(bf16[3072,384]{0,1:T(8,128)(2,1)} %copy.7) | copy-start | bytes 7077892
Sparse Core Ops, SparseCore 0:
  9.2 30.0 all-gather.2
  43.9 50.6 all-gather.4
where the time goes:
time: 108 us
  waiting for transfers between devices  79.1 us (73%)
  between operations  13.5 us (12%)
  local copies, waits for them, and re-layouts  6.49 us (6%)
  matrix products  5.19 us (5%)
  other arithmetic  3.24 us (3%)
    all_gather x1, waiting for transfers between devices, body(): lax.all_gather(stacked, 'vir', axis=1, tiled=True)  47.7 us
    all_gather x1, waiting for transfers between devices, body(): gathered = lax.all_gather(amplitudes, 'occ', axis=0, tiled=True)  30.6 us
    dot_general x1, matrix products, body(): jnp.dot(lax.all_gather(stacked, 'vir', axis=1, tiled=True), masked, prefe...  4.88 us
    gather x1, local copies, waits for them, and re-layouts, body(): partner_rows = jnp.take(gathered, partner, axis=0)  3.4 us
    unnamed x11, local copies, waits for them, and re-layouts  2.65 us
  transfers between devices with their start and end apart: 2, of which 2 were waited for; matrix products, arithmetic and copies ran while one was open for 4% of the time, Pallas kernels for 0%

commit v1 on v0

--- a/solution.py
+++ b/solution.py
@@ -4,6 +4,22 @@
 from jax.sharding import PartitionSpec as P
 
 TILE = 128
+
+
+def touch_the_task(arr_in):
+    dev_axis = "occ"
+    nodes = jax.lax.axis_size(dev_axis)
+    z = [(no - 1, no) for no in range(1, nodes)] + [(nodes - 1, 0)]
+    z1 = arr_in
+    fields = [z1]
+    for _ in range(nodes - 1):
+        z1 = jax.lax.ppermute(z1, axis_name=dev_axis, perm=z)
+        fields += [z1]
+    return jnp.roll(
+        jnp.concatenate([*reversed(fields)], axis=0),
+        (jax.lax.axis_index(dev_axis) + 1) * z1.shape[0],
+        axis=0,
+    )
 
 
 def body(amplitudes, integrals, tile_block, pair_mask, partner):
@@ -23,7 +39,7 @@
     )
     masked = masked.reshape(integrals.shape)
     own_count = amplitudes.shape[0]
-    gathered = lax.all_gather(amplitudes, "occ", axis=0, tiled=True)
+    gathered = touch_the_task(amplitudes)
     partner_rows = jnp.take(gathered, partner, axis=0)
     stacked = jnp.concatenate((amplitudes, partner_rows), axis=0)
     pair_sums = jnp.dot(

time: 108 us -> 103 us (0.954)
  waiting for transfers between devices: 79.1 us -> 70.4 us
  starting transfers between devices: 0.04 us -> 3.69 us
    all_gather x1 -> x0, waiting for transfers between devices: 30.6 us -> none  [body(): gathered = lax.all_gather(amplitudes, 'occ', axis=0, tiled=True)]
    ppermute x0 -> x3, waiting for transfers between devices: none -> 23 us  [touch_the_task(): z1 = jax.lax.ppermute(z1, axis_name=dev_axis, perm=z)]
    ppermute x0 -> x3, starting transfers between devices: none -> 3.69 us  [touch_the_task(): z1 = jax.lax.ppermute(z1, axis_name=dev_axis, perm=z)]
    unnamed x11 -> x14, local copies, waits for them, and re-layouts: 2.65 us -> 4.14 us
    gather x1, local copies, waits for them, and re-layouts: 3.4 us -> 2.12 us  [body(): partner_rows = jnp.take(gathered, partner, axis=0)]
  transfers between devices with their start and end apart: 2 -> 4, of which waited for: 2 -> 4; matrix products, arithmetic and copies ran while one was open for 4% -> 4% of each run, Pallas kernels for 0% -> 0%
where the time goes in v1:
time: 103 us
  waiting for transfers between devices  70.4 us (68%)
  between operations  13.5 us (13%)
  local copies, waits for them, and re-layouts  7.06 us (7%)
  matrix products  5.19 us (5%)
  starting transfers between devices  3.69 us (4%)
  other arithmetic  3.24 us (3%)
    all_gather x1, waiting for transfers between devices, body(): lax.all_gather(stacked, 'vir', axis=1, tiled=True)  47.4 us
    ppermute x3, waiting for transfers between devices, touch_the_task(): z1 = jax.lax.ppermute(z1, axis_name=dev_axis, perm=z)  23 us
    dot_general x1, matrix products, body(): jnp.dot(lax.all_gather(stacked, 'vir', axis=1, tiled=True), masked, prefe...  4.88 us
    unnamed x14, local copies, waits for them, and re-layouts  4.14 us
    ppermute x3, starting transfers between devices, touch_the_task(): z1 = jax.lax.ppermute(z1, axis_name=dev_axis, perm=z)  3.69 us
    gather x1, local copies, waits for them, and re-layouts, body(): partner_rows = jnp.take(gathered, partner, axis=0)  2.12 us
  transfers between devices with their start and end apart: 4, of which 4 were waited for; matrix products, arithmetic and copies ran while one was open for 4% of the time, Pallas kernels for 0%

profile of v1, /device:TPU:0, one launch (start us, length us, event | category | flops | bytes accessed | tf_op | source)
XLA Modules:
  0.0 103.1 jit_solution(14525994498825459020)
XLA Ops:
  6.5 0.0 all-gather.2.cloned.1.call-start
  6.5 3.0 %collective-permute-start = (bf16[376,384]{1,0:T(8,128)(2,1)}, bf16[376,384]{1,0:T(8,128)(2,1)S(1)}, u32[]{:S(2)}, u32[]{:S(2)}) collective-permute-start(bf16[376,384]{1,0:T(8,128)(2,1)} %param.5), channel_id=1, source_target_pairs={{0,8},{8,16},{16,24},{24,0},{1,9},{9,17},{17,25},{25,1},{2,10},{10... | collective-permute-start | bytes 866312 | tf_op jit(solution)/shard_map/ppermute | solution.py:16
  9.5 8.1 %collective-permute-done = bf16[376,384]{1,0:T(8,128)(2,1)S(1)} collective-permute-done((bf16[376,384]{1,0:T(8,128)(2,1)}, bf16[376,384]{1,0:T(8,128)(2,1)S(1)}, u32[]{:S(2)}, u32[]{:S(2)}) %collective-permute-start) | collective-permute-done | bytes 288800 | tf_op jit(solution)/shard_map/ppermute | solution.py:16
  17.6 0.7 collective-permute-start.1
  18.3 0.7 compare_select_fusion
  19.0 7.5 %collective-permute-done.1 = bf16[376,384]{1,0:T(8,128)(2,1)S(1)} collective-permute-done((bf16[376,384]{1,0:T(8,128)(2,1)S(1)}, bf16[376,384]{1,0:T(8,128)(2,1)S(1)}, u32[]{:S(2)}, u32[]{:S(2)}) %collective-permute-start.1) | collective-permute-done | bytes 288800 | tf_op jit(solution)/shard_map/ppermute | solution.py:16
  26.6 0.0 collective-permute-start.2
  26.6 0.7 compare_and_fusion
  27.3 7.4 %collective-permute-done.2 = bf16[376,384]{1,0:T(8,128)(2,1)S(1)} collective-permute-done((bf16[376,384]{1,0:T(8,128)(2,1)S(1)}, bf16[376,384]{1,0:T(8,128)(2,1)S(1)}, u32[]{:S(2)}, u32[]{:S(2)}) %collective-permute-start.2) | collective-permute-done | bytes 288800 | tf_op jit(solution)/shard_map/ppermute | solution.py:16
  34.8 1.0 constant_dynamic-update-slice_fusion.4
  36.0 0.3 constant_dynamic-slice_fusion
  36.3 2.1 %gather_fusion = bf16[376,384]{1,0:T(8,128)(2,1)S(1)} fusion(bf16[1504,384]{1,0:T(8,128)(2,1)S(1)} %constant_dynamic-slice_fusion, s32[1024]{0:T(1024)S(1)} %pad_clamp_fusion), kind=kCustom, calls=%fused_computation | custom fusion | bytes 579040 | tf_op jit(solution)/shard_map/jit(_take)/gather | solution.py:43
  38.5 0.1 broadcast_select_fusion
  38.6 0.9 pad_maximum_fusion
  39.5 0.0 all-gather.2.cloned.1.call-update
  39.5 0.0 copy-start.2
  39.5 0.0 copy-start.1
  39.5 2.8 %copy.7 = bf16[3072,384]{0,1:T(8,128)(2,1)S(1)} copy(bf16[3072,384]{1,0:T(8,128)(2,1)} %param.6) | data formatting | bytes 4718592 | tf_op args[1]
  42.4 0.1 dynamic_slice.8
  42.5 0.3 fusion.5
  42.8 47.4 %all-gather.2.cloned.1.call-done = bf16[752,3072]{1,0:T(8,128)(2,1)} async-done(((bf16[752,384]{1,0:T(8,128)(2,1)}), bf16[752,3072]{1,0:T(8,128)(2,1)}) %all-gather.2.cloned.1.call-update) | async-done | bytes 4620304 | tf_op jit(solution)/shard_map/all_gather | solution.py:46
  90.2 0.4 mul.19
  90.5 4.9 %fusion = f32[752,384]{1,0:T(8,128)S(1)} fusion(bf16[752,3072]{1,0:T(8,128)(2,1)} %all-gather.2.cloned.1.call-done, bf16[3072,384]{0,1:T(8,128)(2,1)S(1)} %copy.7, bf16[48,8,24,128]{3,2,1,0:T(8,128)(2,1)S(1)} %bitcast.8), kind=kOutput, calls=%fused_computation.2 | convolution fusion | flops 1775370240 | bytes 10493952 | tf_op jit(solution)/shard_map/dot_general | solution.py:45
  95.4 0.9 slice_subtract_fusion
  (12 shorter events, 0.3 us)
Async XLA Ops:
  6.5 29.4 %copy-start = (bf16[376,384]{1,0:T(8,128)(2,1)S(1)}, bf16[376,384]{1,0:T(8,128)(2,1)}, u32[]{:S(2)}) copy-start(bf16[376,384]{1,0:T(8,128)(2,1)} %param.5) | copy-start | bytes 866308
  6.5 83.6 %all-gather.2.cloned.1.call-start = ((), (), s32[]{:S(2)}) async-start(), calls=%async_computation | async-start | bytes 5197824 | tf_op jit(solution)/shard_map/all_gather | solution.py:46
  6.5 11.1 %collective-permute-start = (bf16[376,384]{1,0:T(8,128)(2,1)}, bf16[376,384]{1,0:T(8,128)(2,1)S(1)}, u32[]{:S(2)}, u32[]{:S(2)}) collective-permute-start(bf16[376,384]{1,0:T(8,128)(2,1)} %param.5), channel_id=1, source_target_pairs={{0,8},{8,16},{16,24},{24,0},{1,9},{9,17},{17,25},{25,1},{2,10},{10... | collective-permute-start | bytes 866312 | tf_op jit(solution)/shard_map/ppermute | solution.py:16
  17.6 8.9 %collective-permute-start.1 = (bf16[376,384]{1,0:T(8,128)(2,1)S(1)}, bf16[376,384]{1,0:T(8,128)(2,1)S(1)}, u32[]{:S(2)}, u32[]{:S(2)}) collective-permute-start(bf16[376,384]{1,0:T(8,128)(2,1)S(1)} %collective-permute-done), channel_id=1, source_target_pairs={{0,8},{8,16},{16,24},{24,0},{1,9},{9,17},{17,25},{25,1},{2,10},{10... | collective-permute-start | bytes 866312 | tf_op jit(solution)/shard_map/ppermute | solution.py:16
  26.6 8.1 %collective-permute-start.2 = (bf16[376,384]{1,0:T(8,128)(2,1)S(1)}, bf16[376,384]{1,0:T(8,128)(2,1)S(1)}, u32[]{:S(2)}, u32[]{:S(2)}) collective-permute-start(bf16[376,384]{1,0:T(8,128)(2,1)S(1)} %collective-permute-done.1), channel_id=1, source_target_pairs={{0,8},{8,16},{16,24},{24,0},{1,9},{9,17},{17,25},{25,1},{2,10},{10... | collective-permute-start | bytes 866312 | tf_op jit(solution)/shard_map/ppermute | solution.py:16
  39.5 2.9 %copy-start.2 = (s32[24]{0:T(128)S(1)}, s32[24]{0:T(128)}, u32[]{:S(2)}) copy-start(s32[24]{0:T(128)} %param.7) | copy-start | bytes 292
  39.5 3.0 %copy-start.1 = (s32[6,6]{1,0:T(8,128)S(1)}, s32[6,6]{1,0:T(8,128)}, u32[]{:S(2)}) copy-start(s32[6,6]{1,0:T(8,128)} %param.8) | copy-start | bytes 436
Sparse Core Ops, SparseCore 0:
  39.6 50.5 all-gather.1
